TPU v7x, 256 devices: a whole 4x4x8 slice. The times are simulated.
256 devices in a mesh: fgrp: 8 (over z), tile: 16 (over y_lo, x, core), pol: 2 (over y_hi).
Axes of the slice: x: 4, y: 4 (y_hi: 2, y_lo: 2; y = y_hi * 2 + y_lo), z: 8, core: 2. Of those that a mesh axis runs over, the one named last changes fastest.
Arguments:
- voltages: bfloat16 [2, 2048, 131072], P(None, ('tile', 'pol'), 'fgrp'), may hold values from -4 to 4
- gains: float32 [2, 2048, 64], P(None, ('tile', 'pol')), may hold values from -4 to 4
Outputs:
- visibilities: float32 [64, 2, 2048, 2048], P('fgrp', None, ('tile', 'pol'))
All inputs are finite; a program needn't handle non-finite values.
Results may differ from a plain program's by a relative error of at most 0.0039.
Values may be sent and summed in bfloat16 or wider, within the bound.
A program may use at most 128 MiB of HBM per device.

v0:
```python
import math

import jax
import jax.numpy as jnp
from jax import lax
from jax.sharding import PartitionSpec as P

NFFT = 4096
TAPS = 4


def shifted(shard, axis, by):
    length = lax.axis_size(axis)
    pairs = [(i, i + by) for i in range(length) if 0 <= i + by < length]
    return lax.ppermute(shard, axis, pairs)


def make_taps(tap_count, length):
    span_total = tap_count * length
    position = jnp.arange(span_total, dtype=jnp.int32).astype(jnp.float32)
    centred = (position - span_total / 2 + 0.5) / length
    window = 0.5 - 0.5 * jnp.cos(2.0 * math.pi * (position + 0.5) / span_total)
    return (jnp.sinc(centred) * window).reshape(tap_count, length)


def dft_table(length, channels):
    sample = jnp.arange(length, dtype=jnp.int32)
    column = jnp.arange(channels, dtype=jnp.int32)
    phases = sample[:, None] * column[None, :] % length
    angles = phases.astype(jnp.float32) * (2.0 * math.pi / length)
    return jnp.concatenate([jnp.cos(angles), jnp.sin(angles)], axis=1) / math.sqrt(length)


def filter_sum(padded, filter_taps, spectra_count):
    result = filter_taps[0] * padded[:, :, 0:spectra_count, :].astype(jnp.float32)
    for tap_index in range(1, filter_taps.shape[0]):
        result = result + filter_taps[tap_index] * padded[
            :, :, tap_index : tap_index + spectra_count, :
        ].astype(jnp.float32)
    return result


def transform(filtered, table, channels):
    inputs_count = filtered.shape[1]
    spectra_count = filtered.shape[2]
    rows_flat = filtered.reshape(2, inputs_count * spectra_count, filtered.shape[3])
    product = jnp.einsum(
        "prk,kq->prq",
        rows_flat,
        table,
        precision=lax.Precision.HIGHEST,
        preferred_element_type=jnp.float32,
    )
    real_part = product[0, :, :channels] + product[1, :, channels:]
    imag_part = product[1, :, :channels] - product[0, :, channels:]
    return (
        real_part.reshape(inputs_count, spectra_count, channels),
        imag_part.reshape(inputs_count, spectra_count, channels),
    )


def gain_product(real_part, imag_part, gain_block):
    gain_real = gain_block[0][:, None, :]
    gain_imag = gain_block[1][:, None, :]
    out_real = gain_real * real_part - gain_imag * imag_part
    out_imag = gain_real * imag_part + gain_imag * real_part
    return jnp.stack([out_real, out_imag])


def apply_gain(real_part, imag_part, gain_block):
    return gain_product(real_part, imag_part, gain_block).astype(jnp.bfloat16)


def correlate(own_rows, block_cols, norm_factor):
    real_sum = jnp.einsum(
        "csi,csj->cij", own_rows[0], block_cols[0], preferred_element_type=jnp.float32
    ) + jnp.einsum("csi,csj->cij", own_rows[1], block_cols[1], preferred_element_type=jnp.float32)
    imag_sum = jnp.einsum(
        "csi,csj->cij", own_rows[1], block_cols[0], preferred_element_type=jnp.float32
    ) - jnp.einsum("csi,csj->cij", own_rows[0], block_cols[1], preferred_element_type=jnp.float32)
    return jnp.stack([real_sum, imag_sum], axis=1) * norm_factor


def body(voltages, gains):
    inputs_here = voltages.shape[1]
    frames_here = voltages.shape[2] // NFFT
    channels = gains.shape[2]
    history = TAPS - 1
    frames = voltages.reshape(2, inputs_here, frames_here, NFFT)
    filter_taps = make_taps(TAPS, NFFT)
    table = dft_table(NFFT, channels)
    norm_factor = 1.0 / math.sqrt(frames_here * lax.axis_size("fgrp"))
    earlier = shifted(frames[:, :, frames_here - history :, :], "fgrp", 1)
    padded = jnp.concatenate([earlier, frames], axis=2)
    real_part, imag_part = transform(filter_sum(padded, filter_taps, frames_here), table, channels)
    spectra = jnp.transpose(apply_gain(real_part, imag_part, gains), (0, 3, 2, 1))
    turned = lax.all_to_all(spectra, "fgrp", split_axis=1, concat_axis=2, tiled=True)
    return correlate(
        turned, lax.all_gather(turned, ("tile", "pol"), axis=3, tiled=True), norm_factor
    )


def solution(mesh):
    placed = (P(None, ("tile", "pol"), "fgrp"), P(None, ("tile", "pol"), None))
    return jax.shard_map(
        body,
        mesh=mesh,
        in_specs=placed,
        out_specs=P("fgrp", None, ("tile", "pol"), None),
        check_vma=False,
    )
```

profile of v0, /device:TPU:1, one launch (start us, length us, event | category | flops | bytes accessed | tf_op | source)
XLA Modules:
  0.0 272.1 jit_solution(8433359654288791246)
XLA Ops:
  6.5 7.8 %reshape.101 = bf16[2,64,4,4096]{3,2,1,0:T(4,128)(2,1)} reshape(bf16[2,64,16384]{2,1,0:T(8,128)(2,1)} %param.2) | data formatting | bytes 8388608 | tf_op jit(solution)/shard_map/reshape | solution.py:89
  14.3 4.7 %slice.83 = bf16[2,64,3,4096]{3,2,1,0:T(4,128)(2,1)S(1)} slice(bf16[2,64,4,4096]{3,2,1,0:T(4,128)(2,1)} %reshape.101), slice={[0:2], [0:64], [1:4], [0:4096]} | slice | bytes 6291456 | tf_op jit(solution)/shard_map/slice | solution.py:93
  19.1 2.3 copy.42
  21.4 4.7 %collective-permute-start = (bf16[2,64,3,4096]{3,1,2,0:T(8,128)(2,1)S(1)}, bf16[2,64,3,4096]{3,1,2,0:T(8,128)(2,1)S(1)}, u32[]{:S(2)}, u32[]{:S(2)}) collective-permute-start(bf16[2,64,3,4096]{3,1,2,0:T(8,128)(2,1)S(1)} %copy.42), channel_id=1, source_target_pairs={{0,32},{32,64},{64,96},{96,128},{128,160},{160,192},{192,224},{1,3... | collective-permute-start | bytes 9437192 | tf_op jit(solution)/shard_map/ppermute | solution.py:15
  26.1 0.3 fusion.27
  26.5 4.1 %fusion.21 = (f32[4096,64]{0,1:T(8,128)S(1)}, f32[4096,64]{0,1:T(8,128)S(1)}) fusion(), kind=kLoop, calls=%fused_computation.33 | loop fusion | flops 3670016 | bytes 2097152 | tf_op jit(solution)/shard_map/sin | solution.py:31
  30.5 62.0 %collective-permute-done = bf16[2,64,3,4096]{3,1,2,0:T(8,128)(2,1)S(1)} collective-permute-done((bf16[2,64,3,4096]{3,1,2,0:T(8,128)(2,1)S(1)}, bf16[2,64,3,4096]{3,1,2,0:T(8,128)(2,1)S(1)}, u32[]{:S(2)}, u32[]{:S(2)}) %collective-permute-start) | collective-permute-done | bytes 3145760 | tf_op jit(solution)/shard_map/ppermute | solution.py:15
  92.5 2.7 copy.43
  95.2 13.1 %multiply_add_fusion = f32[2,64,4,4096]{3,2,1,0:T(4,128)S(1)} fusion(bf16[2,64,4,4096]{3,2,1,0:T(4,128)(2,1)S(1)} %copy-done, bf16[2,64,3,4096]{3,2,1,0:T(4,128)(2,1)S(1)} %copy.43, f32[4096]{0:T(1024)S(1)} %get-tuple-element.16, f32[4096]{0:T(1024)S(1)} %get-tuple-element.17, f32[4096]{0:T(1024)S(1)} %get-tuple-element.18, f32[4096]{0:T(1024)S(1)} %get-tuple-element.15), kind=kLoop, calls=%fused_computation.7 | loop fusion | flops 41943040 | bytes 15794176 | tf_op jit(solution)/shard_map/add | solution.py:37
  108.3 7.7 %copy.44 = f32[2,64,4,4096]{3,0,2,1:T(2,128)S(1)} copy(f32[2,64,4,4096]{3,2,1,0:T(4,128)S(1)} %multiply_add_fusion) | data formatting | bytes 16777216 | tf_op jit(solution)/shard_map/add | solution.py:37
  116.1 13.6 %fusion = f32[2,256,128]{1,2,0:T(8,128)S(1)} fusion(f32[2,256,4096]{2,0,1:T(2,128)S(1)} %bitcast.40, f32[4096,64]{0,1:T(8,128)S(1)} %get-tuple-element.19, f32[4096,64]{0,1:T(8,128)S(1)} %get-tuple-element.20), kind=kOutput, calls=%fused_computation.5 | convolution fusion | flops 3222274048 | bytes 10747904 | tf_op jit(solution)/shard_map/prk,kq->prq/dot_general | solution.py:47
  129.7 0.1 copy.46
  129.8 0.1 copy.47
  129.9 0.1 subtract_convert_fusion
  130.0 0.4 maximum_bitcast_fusion
  130.3 0.1 copy.48
  130.5 0.2 reshape.104
  130.6 17.1 %all_to_all.18 = bf16[8,2,2048]{2,1,0:T(2,128)(2,1)S(1)} all-to-all(bf16[8,2,2048]{2,1,0:T(2,128)(2,1)S(1)} %reshape.104), channel_id=1, replica_groups=mesh['fgrp'=8,'tile'=16,'pol'=2] {'fgrp'}, dimensions={0} | all-to-all | bytes 131072 | tf_op jit(solution)/shard_map/all_to_all | solution.py:97
  147.7 0.1 reshape.105
  147.9 1.0 copy.52
  148.9 0.1 copy.50
  149.0 0.1 copy.54
  149.1 92.7 %all-gather.2.cloned.1.call-done = bf16[2,8,32,2048]{2,1,0,3:T(8,128)(2,1)} async-done(((bf16[2,8,32,64]{2,1,0,3:T(8,128)(2,1)}), bf16[2,8,32,2048]{2,1,0,3:T(8,128)(2,1)}) %all-gather.2.cloned.1.call-update) | async-done | bytes 2097168 | tf_op jit(solution)/shard_map/all_gather | solution.py:99
  241.7 5.8 %fusion.38 = (bf16[1,8,32,2048]{2,1,0,3:T(8,128)(2,1)}, bf16[1,8,32,2048]{2,1,0,3:T(8,128)(2,1)}) fusion(bf16[2,8,32,2048]{2,1,0,3:T(8,128)(2,1)} %all-gather.2.cloned.1.call-done), kind=kLoop, calls=%fused_computation.69 | loop fusion | bytes 4194304 | tf_op jit(solution)/shard_map/slice | solution.py:77
  247.6 4.4 %copy.57 = bf16[1,8,32,2048]{3,2,1,0:T(8,128)(2,1)S(1)} copy(bf16[1,8,32,2048]{2,1,0,3:T(8,128)(2,1)} %get-tuple-element.6) | data formatting | bytes 2097152
  252.0 4.4 %copy.58 = bf16[1,8,32,2048]{3,2,1,0:T(8,128)(2,1)S(1)} copy(bf16[1,8,32,2048]{2,1,0,3:T(8,128)(2,1)} %get-tuple-element.5) | data formatting | bytes 2097152
  256.4 0.8 fusion.15
  257.2 0.7 fusion.13
  257.9 0.8 add_bitcast_fusion
  258.7 0.8 subtract_bitcast_fusion
  259.5 1.8 maximum_multiply_fusion
  261.3 4.0 %copy.56 = f32[8,2,64,2048]{3,2,1,0:T(8,128)} copy(f32[8,2,64,2048]{3,2,0,1:T(8,128)S(1)} %maximum_multiply_fusion) | data formatting | bytes 16777216 | tf_op jit(solution)/shard_map/mul | solution.py:81
  (12 shorter events, 0.1 us)
Async XLA Ops:
  6.5 235.2 %all-gather.2.cloned.1.call-start = ((), (), s32[]{:S(2)}) async-start(), calls=%async_computation.1 | async-start | bytes 8650752 | tf_op jit(solution)/shard_map/all_gather | solution.py:99
  14.3 12.1 %copy-start.1 = (f32[2,64,64]{2,1,0:T(8,128)S(1)}, f32[2,64,64]{2,1,0:T(8,128)}, u32[]{:S(2)}) copy-start(f32[2,64,64]{2,1,0:T(8,128)} %param.3) | copy-start | bytes 98308
  19.1 76.1 %copy-start = (bf16[2,64,4,4096]{3,2,1,0:T(4,128)(2,1)S(1)}, bf16[2,64,4,4096]{3,2,1,0:T(4,128)(2,1)}, u32[]{:S(2)}) copy-start(bf16[2,64,4,4096]{3,2,1,0:T(4,128)(2,1)} %reshape.101) | copy-start | bytes 12582916
  21.4 71.1 %collective-permute-start = (bf16[2,64,3,4096]{3,1,2,0:T(8,128)(2,1)S(1)}, bf16[2,64,3,4096]{3,1,2,0:T(8,128)(2,1)S(1)}, u32[]{:S(2)}, u32[]{:S(2)}) collective-permute-start(bf16[2,64,3,4096]{3,1,2,0:T(8,128)(2,1)S(1)} %copy.42), channel_id=1, source_target_pairs={{0,32},{32,64},{64,96},{96,128},{128,160},{160,192},{192,224},{1,3... | collective-permute-start | bytes 9437192 | tf_op jit(solution)/shard_map/ppermute | solution.py:15
Sparse Core Ops, SparseCore 0:
  149.0 92.6 all-gather.1
where the time goes:
time: 273 us; the launch traced here: 272 us
  waiting for transfers between devices  155 us (57%)
  local copies, waits for them, and re-layouts  45.7 us (17%)
  other arithmetic  19.8 us (7%)
  blocking collectives  17.1 us (6%)
  matrix products  16.6 us (6%)
  between operations  13.6 us (5%)
  starting transfers between devices  4.74 us (2%)
    all_gather x1, waiting for transfers between devices, body(): lax.all_gather(turned, ('tile', 'pol'), axis=3, tiled=True)  92.7 us
    ppermute x1, waiting for transfers between devices, shifted(): return lax.ppermute(shard, axis, pairs)  62 us
    all_to_all x1, blocking collectives, body(): lax.all_to_all(spectra, 'fgrp', split_axis=1, concat_axis=2, tiled=True)  17.1 us
    dot_general x1, matrix products, transform(): jnp.einsum('prk,kq->prq', rows_flat, table, precision=lax.Precision.HIGHE...  13.6 us
    add x1, other arithmetic, filter_sum(): result + filter_taps[tap_index] * padded[:, :, tap_index:tap_index + spec...  13.1 us
    unnamed x8, local copies, waits for them, and re-layouts  9.15 us
    reshape x1, local copies, waits for them, and re-layouts, body(): frames = voltages.reshape(2, inputs_here, frames_here, NFFT)  7.81 us
    add x1, local copies, waits for them, and re-layouts, filter_sum(): result + filter_taps[tap_index] * padded[:, :, tap_index:tap_index + spec...  7.73 us
  transfers between devices with their start and end apart: 2, of which 2 were waited for; matrix products, arithmetic and copies ran while one was open for 2% of the time, Pallas kernels for 0%

commit v1 on v0

v1 whole, which is shorter than its diff:
```python
import functools
import math

import jax
import jax.numpy as jnp
import numpy as np
from jax import lax
from jax.experimental import pallas as pl
from jax.experimental.pallas import tpu as pltpu
from jax.sharding import PartitionSpec as P

NFFT = 4096
TAPS = 4
MESH = pl.DeviceIdType.MESH


def tap_table():
    total = TAPS * NFFT
    n = np.arange(total, dtype=np.float64)
    x = (n - total / 2 + 0.5) / NFFT
    window = 0.5 - 0.5 * np.cos(2.0 * np.pi * (n + 0.5) / total)
    taps = np.sinc(x) * window / math.sqrt(NFFT)
    return taps.reshape(TAPS, NFFT).astype(np.float32)


def rotation_table():
    k = np.arange(NFFT, dtype=np.int64)
    m = np.arange(8, dtype=np.int64)
    rows = []
    for step in (1, 8):
        angle = (k[None, :] * (step * m)[:, None] % NFFT) * (2.0 * np.pi / NFFT)
        rows += [np.cos(angle), np.sin(angle)]
    return np.stack(rows).astype(np.float32)


def swap_halves(v):
    return jnp.concatenate([v[:, 64:], v[:, :64]], axis=1)


def spectra_kernel(
    volt, gains, taps, rot, out,
    xbuf, gbuf, tbuf, rbuf, table, acc, sbuf, abuf, own,
    in_sem, a2a_send, a2a_recv, ag_send, ux_recv, vy_recv, pt_recv,
):
    z, tile, pol = lax.axis_index("fgrp"), lax.axis_index("tile"), lax.axis_index("pol")
    depth = 8
    core, x, y = tile % 2, (tile // 2) % 4, pol * 2 + tile // 8
    u, v = x + core * (y - x), y + core * (x - y)

    def plane(u2, v2):
        x2, y2 = u2 + core * (v2 - u2), v2 + core * (u2 - v2)
        return ((y2 % 2) * 4 + x2) * 2 + core, y2 // 2

    def device(u2, v2):
        t2, p2 = plane(u2, v2)
        return {"fgrp": z, "tile": t2, "pol": p2}

    def block(u2, v2):
        t2, p2 = plane(u2, v2)
        return t2 * 2 + p2

    up, um, vp, vm = (u + 1) % 4, (u + 3) % 4, (v + 1) % 4, (v + 3) % 4
    partner = {"fgrp": z, "tile": tile + 1 - 2 * core, "pol": pol}
    ring = [(z + dz) % depth for dz in range(depth)]

    barrier = pltpu.get_barrier_semaphore()
    plane_peers = [device(up, v), device(um, v), device(u, vp), device(u, vm), partner]
    for peer in plane_peers:
        pl.semaphore_signal(barrier, inc=1, device_id=peer, device_id_type=MESH)
    for dz in range(1, depth):
        pl.semaphore_signal(
            barrier, inc=1, device_id={"fgrp": ring[dz], "tile": tile, "pol": pol},
            device_id_type=MESH,
        )

    small = [
        pltpu.make_async_copy(rot, rbuf, in_sem.at[4]),
        pltpu.make_async_copy(taps, tbuf, in_sem.at[5]),
        pltpu.make_async_copy(gains, gbuf, in_sem.at[6]),
    ]
    frames = [
        pltpu.make_async_copy(volt.at[:, :, pl.ds(f * NFFT, NFFT)], xbuf.at[f], in_sem.at[f])
        for f in range(4)
    ]
    for copy in small + frames:
        copy.start()
    for copy in small:
        copy.wait()

    lanes = 256

    def make(i, carry):
        ks = pl.ds(pl.multiple_of(i * lanes, lanes), lanes)
        cb, sb = rbuf[0, :, ks], rbuf[1, :, ks]
        for a in range(0, 8, 2):
            cos, sin = [], []
            for step in (a, a + 1):
                ca, sa = rbuf[2, pl.ds(step, 1), ks], rbuf[3, pl.ds(step, 1), ks]
                cos.append(cb * ca - sb * sa)
                sin.append(sb * ca + cb * sa)
            for part, rows in ((0, cos), (64, sin)):
                value = jnp.concatenate(rows, axis=0)
                for t in range(TAPS):
                    tapped = value * tbuf[pl.ds(t, 1), ks]
                    hi = tapped.astype(jnp.bfloat16)
                    lo = (tapped - hi.astype(jnp.float32)).astype(jnp.bfloat16)
                    table[t, pl.ds(part + a * 8, 16), ks] = hi
                    table[t, pl.ds(128 + part + a * 8, 16), ks] = lo
        return carry

    lax.fori_loop(0, NFFT // lanes, make, 0)
    for copy in frames:
        copy.wait()

    def transform(t, carry):
        acc[t] = lax.dot_general(
            table[t], xbuf[...].reshape(512, NFFT), (((1,), (1,)), ((), ())),
            preferred_element_type=jnp.float32,
        )
        return carry

    lax.fori_loop(0, TAPS, transform, 0)

    lane = lax.broadcasted_iota(jnp.int32, (64, 128), 1)
    sign = jnp.where(lane < 64, 1.0, -1.0).astype(jnp.float32)
    g_re = jnp.transpose(jnp.concatenate([gbuf[0], gbuf[0]], axis=0))
    g_im = jnp.transpose(jnp.concatenate([gbuf[1], gbuf[1]], axis=0)) * -sign
    for j in range(7):
        total = None
        for f in range(4):
            t = f - j + 3
            if 0 <= t < TAPS:
                fs = pl.ds(f * 128, 128)
                term = acc[t, pl.ds(0, 128), fs] + acc[t, pl.ds(128, 128), fs]
                total = term if total is None else total + term
        raw = total[:64] + sign * swap_halves(total[64:])
        gained = g_re * raw + g_im * swap_halves(raw)
        for c in range(depth):
            sbuf[c, j] = gained[8 * c : 8 * c + 8]

    pl.semaphore_wait(barrier, depth + 4)
    turns = []
    for dz in (4, 3, 5, 2, 6, 1, 7):
        turn = pltpu.make_async_remote_copy(
            src_ref=sbuf.at[ring[dz]], dst_ref=abuf.at[z],
            send_sem=a2a_send.at[dz], recv_sem=a2a_recv.at[dz],
            device_id={"fgrp": ring[dz], "tile": tile, "pol": pol}, device_id_type=MESH,
        )
        turn.start()
        turns.append(turn)
    abuf[z] = sbuf[z]
    for turn in turns:
        turn.wait_recv()

    for d in range(depth):
        for j in range(4):
            value = abuf[d, j]
            if d > 0 and j < 3:
                value = value + abuf[d - 1, j + 4]
            own[:, 4 * d + j, :] = value
    mine = block(u, v)
    out[mine] = own[...].astype(jnp.bfloat16)

    started = []

    def send(b, half, recv_sem, to):
        ref = out.at[b] if half is None else out.at[b, pl.ds(4 * half, 4)]
        copy = pltpu.make_async_remote_copy(
            src_ref=ref, dst_ref=ref, send_sem=ag_send.at[len(started)], recv_sem=recv_sem,
            device_id=to, device_id_type=MESH,
        )
        copy.start()
        started.append(copy)

    def arrived(b, half, recv_sem):
        ref = out.at[b] if half is None else out.at[b, pl.ds(4 * half, 4)]
        pltpu.make_async_remote_copy(
            src_ref=ref, dst_ref=ref, send_sem=ag_send.at[0], recv_sem=recv_sem,
            device_id=partner, device_id_type=MESH,
        ).wait_recv()

    columns = [u, um, up, (u + 2) % 4]
    rows = [v, vm, vp, (v + 2) % 4]

    def spread(q, b):
        send(b, None, vy_recv.at[q, 0], device(u, vp))
        send(b, None, vy_recv.at[q, 1], device(u, vm))

    def share(q, r):
        send(block(columns[q], rows[r]), None, pt_recv.at[q, r], partner)

    def pass_on(q):
        b = block(columns[q], vm)
        arrived(b, None, vy_recv.at[q, 0])
        send(b, 0, vy_recv.at[q, 2], device(u, vp))
        share(q, 1)
        b = block(columns[q], vp)
        arrived(b, None, vy_recv.at[q, 1])
        send(b, 1, vy_recv.at[q, 3], device(u, vm))
        share(q, 2)

    def far(q):
        b = block(columns[q], rows[3])
        arrived(b, 0, vy_recv.at[q, 2])
        arrived(b, 1, vy_recv.at[q, 3])
        share(q, 3)

    send(mine, None, ux_recv.at[0], device(up, v))
    send(mine, None, ux_recv.at[1], device(um, v))
    spread(0, mine)
    share(0, 0)
    arrived(block(um, v), None, ux_recv.at[0])
    send(block(um, v), 0, ux_recv.at[2], device(up, v))
    spread(1, block(um, v))
    share(1, 0)
    arrived(block(up, v), None, ux_recv.at[1])
    send(block(up, v), 1, ux_recv.at[3], device(um, v))
    spread(2, block(up, v))
    share(2, 0)
    pass_on(0)
    opposite = block(columns[3], v)
    arrived(opposite, 0, ux_recv.at[2])
    arrived(opposite, 1, ux_recv.at[3])
    spread(3, opposite)
    share(3, 0)
    pass_on(1)
    pass_on(2)
    far(0)
    pass_on(3)
    far(1)
    far(2)
    far(3)
    for q in range(4):
        for r in range(4):
            arrived(mine, None, pt_recv.at[q, r])
    for turn in turns:
        turn.wait_send()
    for copy in started:
        copy.wait_send()


def correlate_kernel(norm, blocks, out):
    m = pl.program_id(0)
    mine = lax.axis_index("tile") * 2 + lax.axis_index("pol")
    count = blocks.shape[0]
    first = lax.broadcasted_iota(jnp.int32, (32, 128), 1) < 64
    a = blocks[mine, m]
    swapped = swap_halves(a)
    lhs = jnp.concatenate([a, jnp.where(first, swapped, -swapped)], axis=0)
    for q in range(0, count, 4):
        tiles = []
        for b in (q, q + 2):
            g, h = blocks[b, m], blocks[b + 1, m]
            re = jnp.where(first, g, swap_halves(h))
            im = jnp.where(first, swap_halves(g), h)
            tiles.append(jnp.concatenate([re, im], axis=0))
        rhs = jnp.concatenate(tiles, axis=1)
        vis = lax.dot_general(
            lhs, rhs, (((0,), (0,)), ((), ())), preferred_element_type=jnp.float32
        ) * norm
        out[0, 0, :, pl.ds(q * 64, 256)] = vis[:64]
        out[0, 1, :, pl.ds(q * 64, 256)] = vis[64:]


def body(voltages, gains):
    inputs, channels = voltages.shape[1], gains.shape[2]
    fgrp = lax.axis_size("fgrp")
    count = lax.axis_size("tile") * lax.axis_size("pol")
    spectra = voltages.shape[2] // NFFT * fgrp
    mine = channels // fgrp
    any_spec = pl.BlockSpec(memory_space=pl.ANY)
    vmem_spec = pl.BlockSpec(memory_space=pltpu.VMEM)
    dma = pltpu.SemaphoreType.DMA
    blocks = pl.pallas_call(
        spectra_kernel,
        out_shape=pltpu.VMEM((count, mine, spectra, 2 * inputs), jnp.bfloat16),
        in_specs=[any_spec] * 4,
        out_specs=vmem_spec,
        scratch_shapes=[
            pltpu.VMEM((4, 2, inputs, NFFT), jnp.bfloat16),
            pltpu.VMEM((2, inputs, channels), jnp.float32),
            pltpu.VMEM((TAPS, NFFT), jnp.float32),
            pltpu.VMEM((4, 8, NFFT), jnp.float32),
            pltpu.VMEM((TAPS, 4 * channels, NFFT), jnp.bfloat16),
            pltpu.VMEM((TAPS, 4 * channels, 8 * inputs), jnp.float32),
            pltpu.VMEM((fgrp, 7, mine, 2 * inputs), jnp.float32),
            pltpu.VMEM((fgrp, 7, mine, 2 * inputs), jnp.float32),
            pltpu.VMEM((mine, spectra, 2 * inputs), jnp.float32),
            dma((7,)), dma((fgrp,)), dma((fgrp,)), dma((40,)), dma((4,)), dma((4, 4)), dma((4, 4)),
        ],
        compiler_params=pltpu.CompilerParams(
            collective_id=0, has_side_effects=True, vmem_limit_bytes=32 * 1024 * 1024
        ),
        name="spectra",
    )(voltages, gains, jnp.asarray(tap_table()), jnp.asarray(rotation_table()))
    return pl.pallas_call(
        functools.partial(correlate_kernel, 1.0 / math.sqrt(spectra)),
        out_shape=jax.ShapeDtypeStruct((mine, 2, inputs, count * inputs), jnp.float32),
        grid=(mine,),
        in_specs=[vmem_spec],
        out_specs=pl.BlockSpec((1, 2, inputs, count * inputs), lambda m: (m, 0, 0, 0)),
        compiler_params=pltpu.CompilerParams(vmem_limit_bytes=16 * 1024 * 1024),
        name="correlate",
    )(blocks)


def solution(mesh):
    return jax.shard_map(
        body,
        mesh=mesh,
        in_specs=(P(None, ("tile", "pol"), "fgrp"), P(None, ("tile", "pol"), None)),
        out_specs=P("fgrp", None, ("tile", "pol"), None),
        check_vma=False,
    )
```

time: 273 us -> 50.2 us (0.18)
  waiting for transfers between devices: 155 us -> 0 us
  Pallas kernels: 0 us -> 45 us
  local copies, waits for them, and re-layouts: 45.7 us -> 4.91 us
  other arithmetic: 19.8 us -> 0 us
  blocking collectives: 17.1 us -> 0 us
  matrix products: 16.6 us -> 0 us
  between operations: 13.6 us -> 0.01 us
  starting transfers between devices: 4.74 us -> 0 us
    all_gather x1 -> x0, waiting for transfers between devices: 92.7 us -> none  [body(): lax.all_gather(turned, ('tile', 'pol'), axis=3, tiled=True)]
    ppermute x1 -> x0, waiting for transfers between devices: 62 us -> none  [shifted(): return lax.ppermute(shard, axis, pairs)]
    pallas_call x0 -> x2, Pallas kernels: none -> 45 us  [the longest x1 39.1 us: body(): pl.pallas_call(spectra_kernel, out_shape=pltpu.VMEM((count, mine, spectra...]
    all_to_all x1 -> x0, blocking collectives: 17.1 us -> none  [body(): lax.all_to_all(spectra, 'fgrp', split_axis=1, concat_axis=2, tiled=True)]
    dot_general x5 -> x0, matrix products: 16.6 us -> none  [the longest x1 13.6 us: transform(): jnp.einsum('prk,kq->prq', rows_flat, table, precision=lax.Precision.HIGHE...]
    add x1 -> x0, other arithmetic: 13.1 us -> none  [filter_sum(): result + filter_taps[tap_index] * padded[:, :, tap_index:tap_index + spec...]
    slice x7 -> x0, local copies, waits for them, and re-layouts: 12.9 us -> none  [the longest x2 6.99 us: body(): earlier = shifted(frames[:, :, frames_here - history:, :], 'fgrp', 1)]
    add x2 -> x0, local copies, waits for them, and re-layouts: 7.82 us -> none  [the longest x1 7.73 us: filter_sum(): result + filter_taps[tap_index] * padded[:, :, tap_index:tap_index + spec...]
  transfers between devices with their start and end apart: 2 -> 0, of which waited for: 2 -> 0; matrix products, arithmetic and copies ran while one was open for 2% -> 0% of each run, Pallas kernels for 0% -> 0%
where the time goes in v1:
time: 50.2 us; the launch traced here: 49.9 us
  Pallas kernels  45 us (90%)
  local copies, waits for them, and re-layouts  4.91 us (10%)
    pallas_call x1, Pallas kernels, body(): pl.pallas_call(spectra_kernel, out_shape=pltpu.VMEM((count, mine, spectra...  39.1 us
    pallas_call x1, Pallas kernels, body(): pl.pallas_call(functools.partial(correlate_kernel, 1.0 / math.sqrt(spectr...  5.92 us
    unnamed x8, local copies, waits for them, and re-layouts  4.91 us

profile of v1, /device:TPU:1, one launch (start us, length us, event | category | flops | bytes accessed | tf_op | source)
XLA Modules:
  0.0 49.9 jit_solution(1293828650995694168)
XLA Ops:
  0.0 0.0 copy-start
  0.0 2.2 %copy-done = bf16[2,64,16384]{2,1,0:T(8,128)(2,1)S(1)} copy-done((bf16[2,64,16384]{2,1,0:T(8,128)(2,1)S(1)}, bf16[2,64,16384]{2,1,0:T(8,128)(2,1)}, u32[]{:S(2)}) %copy-start) | copy-done | bytes 4194328
  2.2 0.0 copy-start.1
  2.2 1.0 %copy-done.1 = f32[4,8,4096]{2,1,0:T(8,128)S(1)} copy-done((f32[4,8,4096]{2,1,0:T(8,128)S(1)}, f32[4,8,4096]{2,1,0:T(8,128)}, u32[]{:S(2)}) %copy-start.1) | copy-done | bytes 524312
  3.2 0.0 copy-start.2
  3.2 0.8 %copy-done.2 = f32[2,64,64]{2,1,0:T(8,128)S(1)} copy-done((f32[2,64,64]{2,1,0:T(8,128)S(1)}, f32[2,64,64]{2,1,0:T(8,128)}, u32[]{:S(2)}) %copy-start.2) | copy-done | bytes 32792
  4.1 0.0 copy-start.3
  4.1 0.8 %copy-done.3 = f32[4,4096]{1,0:T(4,128)S(1)} copy-done((f32[4,4096]{1,0:T(4,128)S(1)}, f32[4,4096]{1,0:T(4,128)}, u32[]{:S(2)}) %copy-start.3) | copy-done | bytes 65560
  4.9 39.1 %spectra.1.blocks = bf16[32,8,32,128]{3,2,1,0:T(8,128)(2,1)S(1)} custom-call(bf16[2,64,16384]{2,1,0:T(8,128)(2,1)S(1)} %copy-done, f32[2,64,64]{2,1,0:T(8,128)S(1)} %copy-done.2, f32[4,4096]{1,0:T(4,128)S(1)} %copy-done.3, f32[4,8,4096]{2,1,0:T(8,128)S(1)} %copy-done.1), custom_call_target="tpu_custom_call" | custom-call | tf_op jit(solution)/shard_map/spectra/pallas_call | solution.py:274
  44.0 5.9 %correlate.1 = f32[8,2,64,2048]{3,2,1,0:T(8,128)} custom-call(bf16[32,8,32,128]{3,2,1,0:T(8,128)(2,1)S(1)} %spectra.1.blocks), custom_call_target="tpu_custom_call" | custom-call | tf_op jit(solution)/shard_map/correlate/pallas_call | solution.py:296
Async XLA Ops:
  0.0 2.2 %copy-start = (bf16[2,64,16384]{2,1,0:T(8,128)(2,1)S(1)}, bf16[2,64,16384]{2,1,0:T(8,128)(2,1)}, u32[]{:S(2)}) copy-start(bf16[2,64,16384]{2,1,0:T(8,128)(2,1)} %volt.1) | copy-start | bytes 12582916
  2.2 1.0 %copy-start.1 = (f32[4,8,4096]{2,1,0:T(8,128)S(1)}, f32[4,8,4096]{2,1,0:T(8,128)}, u32[]{:S(2)}) copy-start(f32[4,8,4096]{2,1,0:T(8,128)} %constant.5.clone.rot) | copy-start | bytes 1572868
  3.2 0.8 %copy-start.2 = (f32[2,64,64]{2,1,0:T(8,128)S(1)}, f32[2,64,64]{2,1,0:T(8,128)}, u32[]{:S(2)}) copy-start(f32[2,64,64]{2,1,0:T(8,128)} %gains.1) | copy-start | bytes 98308
  4.1 0.8 %copy-start.3 = (f32[4,4096]{1,0:T(4,128)S(1)}, f32[4,4096]{1,0:T(4,128)}, u32[]{:S(2)}) copy-start(f32[4,4096]{1,0:T(4,128)} %constant.4.clone.taps) | copy-start | bytes 196612

commit v2 on v1

v2 whole, which is shorter than its diff:
```python
import functools
import math

import jax
import jax.numpy as jnp
import numpy as np
from jax import lax
from jax.experimental import pallas as pl
from jax.experimental.pallas import tpu as pltpu
from jax.sharding import PartitionSpec as P

NFFT = 4096
TAPS = 4
MESH = pl.DeviceIdType.MESH


def tap_table():
    total = TAPS * NFFT
    n = np.arange(total, dtype=np.float64)
    x = (n - total / 2 + 0.5) / NFFT
    window = 0.5 - 0.5 * np.cos(2.0 * np.pi * (n + 0.5) / total)
    taps = np.sinc(x) * window / math.sqrt(NFFT)
    return taps.reshape(TAPS, NFFT).astype(np.float32)


def rotation_table():
    k = np.arange(NFFT, dtype=np.int64)
    m = np.arange(8, dtype=np.int64)
    rows = []
    for step in (1, 8):
        angle = (k[None, :] * (step * m)[:, None] % NFFT) * (2.0 * np.pi / NFFT)
        rows += [np.cos(angle), np.sin(angle)]
    return np.stack(rows).astype(np.float32)


def swap_halves(v):
    return jnp.concatenate([v[:, 64:], v[:, :64]], axis=1)


def spectra_kernel(
    volt, gains, taps, rot, out,
    xbuf, gbuf, tbuf, rbuf, table, acc, sbuf, abuf, own,
    in_sem, a2a_send, a2a_recv, ag_send, ux_recv, vy_recv, pt_recv,
):
    z, tile, pol = lax.axis_index("fgrp"), lax.axis_index("tile"), lax.axis_index("pol")
    depth = 8
    core, x, y = tile % 2, (tile // 2) % 4, pol * 2 + tile // 8
    u, v = x + core * (y - x), y + core * (x - y)

    def plane(u2, v2):
        x2, y2 = u2 + core * (v2 - u2), v2 + core * (u2 - v2)
        return ((y2 % 2) * 4 + x2) * 2 + core, y2 // 2

    def device(u2, v2):
        t2, p2 = plane(u2, v2)
        return {"fgrp": z, "tile": t2, "pol": p2}

    def block(u2, v2):
        t2, p2 = plane(u2, v2)
        return t2 * 2 + p2

    partner = {"fgrp": z, "tile": tile + 1 - 2 * core, "pol": pol}
    ring = [(z + dz) % depth for dz in range(depth)]

    barrier = pltpu.get_barrier_semaphore()
    plane_peers = [device((u + d) % 4, v) for d in (1, 2, 3)] + [device(u, (v + d) % 4) for d in (1, 2, 3)]
    plane_peers.append(partner)
    for peer in plane_peers:
        pl.semaphore_signal(barrier, inc=1, device_id=peer, device_id_type=MESH)
    for dz in range(1, depth):
        pl.semaphore_signal(
            barrier, inc=1, device_id={"fgrp": ring[dz], "tile": tile, "pol": pol},
            device_id_type=MESH,
        )

    small = [
        pltpu.make_async_copy(rot, rbuf, in_sem.at[4]),
        pltpu.make_async_copy(taps, tbuf, in_sem.at[5]),
        pltpu.make_async_copy(gains, gbuf, in_sem.at[6]),
    ]
    frames = [
        pltpu.make_async_copy(volt.at[:, :, pl.ds(f * NFFT, NFFT)], xbuf.at[f], in_sem.at[f])
        for f in range(4)
    ]
    for copy in small + frames:
        copy.start()
    for copy in small:
        copy.wait()

    lanes = 256

    def make(i, carry):
        ks = pl.ds(pl.multiple_of(i * lanes, lanes), lanes)
        cb, sb = rbuf[0, :, ks], rbuf[1, :, ks]
        for a in range(0, 8, 2):
            cos, sin = [], []
            for step in (a, a + 1):
                ca, sa = rbuf[2, pl.ds(step, 1), ks], rbuf[3, pl.ds(step, 1), ks]
                cos.append(cb * ca - sb * sa)
                sin.append(sb * ca + cb * sa)
            for part, rows in ((0, cos), (64, sin)):
                value = jnp.concatenate(rows, axis=0)
                high, low = pl.ds(part + a * 8, 16), pl.ds(128 + part + a * 8, 16)
                for t in (1, 2):
                    tapped = value * tbuf[pl.ds(t, 1), ks]
                    rounded = tapped.astype(jnp.bfloat16)
                    table[t - 1, high, ks] = rounded
                    table[t - 1, low, ks] = (tapped - rounded.astype(jnp.float32)).astype(jnp.bfloat16)
                table[2, high, ks] = (value * tbuf[pl.ds(0, 1), ks]).astype(jnp.bfloat16)
                table[2, low, ks] = (value * tbuf[pl.ds(3, 1), ks]).astype(jnp.bfloat16)
        return carry

    lax.fori_loop(0, NFFT // lanes, make, 0)
    for copy in frames:
        copy.wait()

    def transform(part, carry):
        acc[part] = lax.dot_general(
            table[part], xbuf[...].reshape(512, NFFT), (((1,), (1,)), ((), ())),
            preferred_element_type=jnp.float32,
        )
        return carry

    lax.fori_loop(0, 3, transform, 0)

    lane = lax.broadcasted_iota(jnp.int32, (64, 128), 1)
    sign = jnp.where(lane < 64, 1.0, -1.0).astype(jnp.float32)
    g_re = jnp.transpose(jnp.concatenate([gbuf[0], gbuf[0]], axis=0))
    g_im = jnp.transpose(jnp.concatenate([gbuf[1], gbuf[1]], axis=0)) * -sign
    for j in range(7):
        total = None
        for f in range(4):
            t = f - j + 3
            if 0 <= t < TAPS:
                fs = pl.ds(f * 128, 128)
                if t in (1, 2):
                    term = acc[t - 1, pl.ds(0, 128), fs] + acc[t - 1, pl.ds(128, 128), fs]
                else:
                    term = acc[2, pl.ds(128 if t else 0, 128), fs]
                total = term if total is None else total + term
        raw = total[:64] + sign * swap_halves(total[64:])
        gained = g_re * raw + g_im * swap_halves(raw)
        for c in range(depth):
            sbuf[c, j] = gained[8 * c : 8 * c + 8]

    pl.semaphore_wait(barrier, depth + 6)
    turns = []
    for dz in (4, 3, 5, 2, 6, 1, 7):
        turn = pltpu.make_async_remote_copy(
            src_ref=sbuf.at[ring[dz]], dst_ref=abuf.at[z],
            send_sem=a2a_send.at[dz], recv_sem=a2a_recv.at[dz],
            device_id={"fgrp": ring[dz], "tile": tile, "pol": pol}, device_id_type=MESH,
        )
        turn.start()
        turns.append(turn)
    abuf[z] = sbuf[z]
    for turn in turns:
        turn.wait_recv()

    for d in range(depth):
        for j in range(4):
            value = abuf[d, j]
            if d > 0 and j < 3:
                value = value + abuf[d - 1, j + 4]
            own[:, 4 * d + j, :] = value
    mine = block(u, v)
    out[mine] = own[...].astype(jnp.bfloat16)

    started = []
    columns, rows = [u, (u + 3) % 4, (u + 1) % 4, (u + 2) % 4], [v, (v + 3) % 4, (v + 1) % 4, (v + 2) % 4]

    def send(b, recv_sem, to):
        copy = pltpu.make_async_remote_copy(
            src_ref=out.at[b], dst_ref=out.at[b], send_sem=ag_send.at[len(started)],
            recv_sem=recv_sem, device_id=to, device_id_type=MESH,
        )
        copy.start()
        started.append(copy)

    def arrived(b, recv_sem):
        pltpu.make_async_remote_copy(
            src_ref=out.at[b], dst_ref=out.at[b], send_sem=ag_send.at[0],
            recv_sem=recv_sem, device_id=partner, device_id_type=MESH,
        ).wait_recv()

    def spread(q):
        b = block(columns[q], v)
        send(b, vy_recv.at[q, 3], device(u, rows[3]))
        send(b, vy_recv.at[q, 1], device(u, rows[2]))
        send(b, vy_recv.at[q, 2], device(u, rows[1]))
        send(b, pt_recv.at[q, 0], partner)

    send(mine, ux_recv.at[3], device(columns[3], v))
    send(mine, ux_recv.at[1], device(columns[2], v))
    send(mine, ux_recv.at[2], device(columns[1], v))
    spread(0)
    for q in (1, 2, 3):
        arrived(block(columns[q], v), ux_recv.at[q])
        spread(q)
    for q in range(4):
        for r in (1, 2, 3):
            b = block(columns[q], rows[r])
            arrived(b, vy_recv.at[q, r])
            send(b, pt_recv.at[q, r], partner)
    for q in range(4):
        for r in range(4):
            arrived(mine, pt_recv.at[q, r])
    for turn in turns:
        turn.wait_send()
    for copy in started:
        copy.wait_send()


def correlate_kernel(norm, blocks, out, vis, sems):
    mine = lax.axis_index("tile") * 2 + lax.axis_index("pol")
    count, channels = blocks.shape[0], blocks.shape[1]
    first = lax.broadcasted_iota(jnp.int32, (32, 128), 1) < 64

    def write(m, part):
        return pltpu.make_async_copy(vis.at[m, part], out.at[m, part], sems.at[m, part])

    def channel(m, carry):
        a = blocks[mine, m]
        swapped = swap_halves(a)
        lhs = jnp.concatenate([a, jnp.where(first, swapped, -swapped)], axis=0)
        for q in range(0, count, 4):
            tiles = []
            for b in (q, q + 2):
                g, h = blocks[b, m], blocks[b + 1, m]
                re = jnp.where(first, g, swap_halves(h))
                im = jnp.where(first, swap_halves(g), h)
                tiles.append(jnp.concatenate([re, im], axis=0))
            rhs = jnp.concatenate(tiles, axis=1)
            product = lax.dot_general(
                lhs, rhs, (((0,), (0,)), ((), ())), preferred_element_type=jnp.float32
            ) * norm
            vis[m, 0, :, pl.ds(q * 64, 256)] = product[:64]
            vis[m, 1, :, pl.ds(q * 64, 256)] = product[64:]
        write(m, 0).start()
        write(m, 1).start()
        return carry

    lax.fori_loop(0, channels, channel, 0)
    for m in range(channels):
        write(m, 0).wait()
        write(m, 1).wait()


def body(voltages, gains):
    inputs, channels = voltages.shape[1], gains.shape[2]
    fgrp = lax.axis_size("fgrp")
    count = lax.axis_size("tile") * lax.axis_size("pol")
    spectra = voltages.shape[2] // NFFT * fgrp
    mine = channels // fgrp
    any_spec = pl.BlockSpec(memory_space=pltpu.HBM)
    vmem_spec = pl.BlockSpec(memory_space=pltpu.VMEM)
    dma = pltpu.SemaphoreType.DMA
    blocks = pl.pallas_call(
        spectra_kernel,
        out_shape=pltpu.VMEM((count, mine, spectra, 2 * inputs), jnp.bfloat16),
        in_specs=[any_spec] * 4,
        out_specs=vmem_spec,
        scratch_shapes=[
            pltpu.VMEM((4, 2, inputs, NFFT), jnp.bfloat16),
            pltpu.VMEM((2, inputs, channels), jnp.float32),
            pltpu.VMEM((TAPS, NFFT), jnp.float32),
            pltpu.VMEM((4, 8, NFFT), jnp.float32),
            pltpu.VMEM((3, 4 * channels, NFFT), jnp.bfloat16),
            pltpu.VMEM((3, 4 * channels, 8 * inputs), jnp.float32),
            pltpu.VMEM((fgrp, 7, mine, 2 * inputs), jnp.float32),
            pltpu.VMEM((fgrp, 7, mine, 2 * inputs), jnp.float32),
            pltpu.VMEM((mine, spectra, 2 * inputs), jnp.float32),
            dma((7,)), dma((fgrp,)), dma((fgrp,)), dma((40,)), dma((4,)), dma((4, 4)), dma((4, 4)),
        ],
        compiler_params=pltpu.CompilerParams(
            collective_id=0, has_side_effects=True, vmem_limit_bytes=32 * 1024 * 1024
        ),
        name="spectra",
    )(*[
        pltpu.with_memory_space_constraint(operand, pltpu.HBM)
        for operand in (voltages, gains, jnp.asarray(tap_table()), jnp.asarray(rotation_table()))
    ])
    vis_shape = (mine, 2, inputs, count * inputs)
    return pl.pallas_call(
        functools.partial(correlate_kernel, 1.0 / math.sqrt(spectra)),
        out_shape=jax.ShapeDtypeStruct(vis_shape, jnp.float32),
        in_specs=[vmem_spec],
        out_specs=any_spec,
        scratch_shapes=[pltpu.VMEM(vis_shape, jnp.float32), dma((mine, 2))],
        compiler_params=pltpu.CompilerParams(vmem_limit_bytes=16 * 1024 * 1024),
        name="correlate",
    )(blocks)


def solution(mesh):
    return jax.shard_map(
        body,
        mesh=mesh,
        in_specs=(P(None, ("tile", "pol"), "fgrp"), P(None, ("tile", "pol"), None)),
        out_specs=P("fgrp", None, ("tile", "pol"), None),
        check_vma=False,
    )
```

time: 50.2 us -> 40.9 us (0.81)
  local copies, waits for them, and re-layouts: 4.91 us -> 0 us
  Pallas kernels: 45 us -> 40.9 us
    unnamed x8 -> x0, local copies, waits for them, and re-layouts: 4.91 us -> none
    pallas_call x1, Pallas kernels: 39.1 us -> 36.6 us  [body(): pl.pallas_call(spectra_kernel, out_shape=pltpu.VMEM((count, mine, spectra...]
    pallas_call x1, Pallas kernels: 5.92 us -> 4.24 us  [body(): pl.pallas_call(functools.partial(correlate_kernel, 1.0 / math.sqrt(spectr...]
where the time goes in v2:
time: 40.9 us
  Pallas kernels  40.9 us (100%)
    pallas_call x1, Pallas kernels, body(): pl.pallas_call(spectra_kernel, out_shape=pltpu.VMEM((count, mine, spectra...  36.6 us
    pallas_call x1, Pallas kernels, body(): pl.pallas_call(functools.partial(correlate_kernel, 1.0 / math.sqrt(spectr...  4.24 us

profile of v2, /device:TPU:1, one launch (start us, length us, event | category | flops | bytes accessed | tf_op | source)
XLA Modules:
  0.0 40.9 jit_solution(8196462890405156324)
XLA Ops:
  0.0 36.6 %spectra.1.blocks = bf16[32,8,32,128]{3,2,1,0:T(8,128)(2,1)S(1)} custom-call(bf16[2,64,16384]{2,1,0:T(8,128)(2,1)} %volt.1, f32[2,64,64]{2,1,0:T(8,128)} %gains.1, f32[4,4096]{1,0:T(4,128)} %constant.4.clone.taps, f32[4,8,4096]{2,1,0:T(8,128)} %constant.5.clone.rot), custom_call_target="tpu_custom_call" | custom-call | tf_op jit(solution)/shard_map/spectra/pallas_call | solution.py:258
  36.6 4.2 %correlate.1 = f32[8,2,64,2048]{3,2,1,0:T(8,128)} custom-call(bf16[32,8,32,128]{3,2,1,0:T(8,128)(2,1)S(1)} %spectra.1.blocks), custom_call_target="tpu_custom_call" | custom-call | tf_op jit(solution)/shard_map/correlate/pallas_call | solution.py:284

commit v3 on v2

--- a/solution.py
+++ b/solution.py
@@ -39,7 +39,7 @@
 
 def spectra_kernel(
     volt, gains, taps, rot, out,
-    xbuf, gbuf, tbuf, rbuf, table, acc, sbuf, abuf, own,
+    xbuf, gbuf, tbuf, rbuf, table, acc, wide_send, wide, thin_send, thin, own,
     in_sem, a2a_send, a2a_recv, ag_send, ux_recv, vy_recv, pt_recv,
 ):
     z, tile, pol = lax.axis_index("fgrp"), lax.axis_index("tile"), lax.axis_index("pol")
@@ -98,70 +98,78 @@
                 ca, sa = rbuf[2, pl.ds(step, 1), ks], rbuf[3, pl.ds(step, 1), ks]
                 cos.append(cb * ca - sb * sa)
                 sin.append(sb * ca + cb * sa)
-            for part, rows in ((0, cos), (64, sin)):
+            for first, rows in ((0, cos), (64, sin)):
                 value = jnp.concatenate(rows, axis=0)
-                high, low = pl.ds(part + a * 8, 16), pl.ds(128 + part + a * 8, 16)
+                row = first + a * 8
                 for t in (1, 2):
                     tapped = value * tbuf[pl.ds(t, 1), ks]
                     rounded = tapped.astype(jnp.bfloat16)
-                    table[t - 1, high, ks] = rounded
-                    table[t - 1, low, ks] = (tapped - rounded.astype(jnp.float32)).astype(jnp.bfloat16)
-                table[2, high, ks] = (value * tbuf[pl.ds(0, 1), ks]).astype(jnp.bfloat16)
-                table[2, low, ks] = (value * tbuf[pl.ds(3, 1), ks]).astype(jnp.bfloat16)
+                    low = tapped - rounded.astype(jnp.float32)
+                    table[pl.ds((t - 1) * 256 + row, 16), ks] = rounded
+                    table[pl.ds((t - 1) * 256 + 128 + row, 16), ks] = low.astype(jnp.bfloat16)
+                for t, base in ((0, 512), (3, 640)):
+                    tapped = value * tbuf[pl.ds(t, 1), ks]
+                    table[pl.ds(base + row, 16), ks] = tapped.astype(jnp.bfloat16)
         return carry
 
     lax.fori_loop(0, NFFT // lanes, make, 0)
     for copy in frames:
         copy.wait()
-
-    def transform(part, carry):
-        acc[part] = lax.dot_general(
-            table[part], xbuf[...].reshape(512, NFFT), (((1,), (1,)), ((), ())),
-            preferred_element_type=jnp.float32,
-        )
-        return carry
-
-    lax.fori_loop(0, 3, transform, 0)
+    acc[...] = lax.dot_general(
+        table[...], xbuf[...].reshape(acc.shape[1], NFFT), (((1,), (1,)), ((), ())),
+        preferred_element_type=jnp.float32,
+    )
 
     lane = lax.broadcasted_iota(jnp.int32, (64, 128), 1)
     sign = jnp.where(lane < 64, 1.0, -1.0).astype(jnp.float32)
     g_re = jnp.transpose(jnp.concatenate([gbuf[0], gbuf[0]], axis=0))
     g_im = jnp.transpose(jnp.concatenate([gbuf[1], gbuf[1]], axis=0)) * -sign
+    thin_of, wide_of = {0: 0, 3: 1, 6: 2}, {1: 0, 2: 1, 4: 2, 5: 3}
     for j in range(7):
         total = None
         for f in range(4):
             t = f - j + 3
             if 0 <= t < TAPS:
                 fs = pl.ds(f * 128, 128)
+                base = (512, 0, 256, 640)[t]
+                term = acc[pl.ds(base, 128), fs]
                 if t in (1, 2):
-                    term = acc[t - 1, pl.ds(0, 128), fs] + acc[t - 1, pl.ds(128, 128), fs]
-                else:
-                    term = acc[2, pl.ds(128 if t else 0, 128), fs]
+                    term = term + acc[pl.ds(base + 128, 128), fs]
                 total = term if total is None else total + term
         raw = total[:64] + sign * swap_halves(total[64:])
         gained = g_re * raw + g_im * swap_halves(raw)
         for c in range(depth):
-            sbuf[c, j] = gained[8 * c : 8 * c + 8]
+            if j in thin_of:
+                thin_send[c, thin_of[j]] = gained[8 * c : 8 * c + 8].astype(jnp.bfloat16)
+            else:
+                wide_send[c, wide_of[j]] = gained[8 * c : 8 * c + 8]
 
     pl.semaphore_wait(barrier, depth + 6)
     turns = []
     for dz in (4, 3, 5, 2, 6, 1, 7):
-        turn = pltpu.make_async_remote_copy(
-            src_ref=sbuf.at[ring[dz]], dst_ref=abuf.at[z],
-            send_sem=a2a_send.at[dz], recv_sem=a2a_recv.at[dz],
-            device_id={"fgrp": ring[dz], "tile": tile, "pol": pol}, device_id_type=MESH,
-        )
-        turn.start()
-        turns.append(turn)
-    abuf[z] = sbuf[z]
+        for k, (mine, theirs) in enumerate(((wide_send, wide), (thin_send, thin))):
+            turn = pltpu.make_async_remote_copy(
+                src_ref=mine.at[ring[dz]], dst_ref=theirs.at[z],
+                send_sem=a2a_send.at[k, dz], recv_sem=a2a_recv.at[k, dz],
+                device_id={"fgrp": ring[dz], "tile": tile, "pol": pol}, device_id_type=MESH,
+            )
+            turn.start()
+            turns.append(turn)
+    wide[z] = wide_send[z]
+    thin[z] = thin_send[z]
     for turn in turns:
         turn.wait_recv()
 
+    def partial(d, j):
+        if j in thin_of:
+            return thin[d, thin_of[j]].astype(jnp.float32)
+        return wide[d, wide_of[j]]
+
     for d in range(depth):
         for j in range(4):
-            value = abuf[d, j]
+            value = partial(d, j)
             if d > 0 and j < 3:
-                value = value + abuf[d - 1, j + 4]
+                value = value + partial(d - 1, j + 4)
             own[:, 4 * d + j, :] = value
     mine = block(u, v)
     out[mine] = own[...].astype(jnp.bfloat16)
@@ -185,14 +193,14 @@
 
     def spread(q):
         b = block(columns[q], v)
-        send(b, vy_recv.at[q, 3], device(u, rows[3]))
         send(b, vy_recv.at[q, 1], device(u, rows[2]))
         send(b, vy_recv.at[q, 2], device(u, rows[1]))
+        send(b, vy_recv.at[q, 3], device(u, rows[3]))
         send(b, pt_recv.at[q, 0], partner)
 
-    send(mine, ux_recv.at[3], device(columns[3], v))
     send(mine, ux_recv.at[1], device(columns[2], v))
     send(mine, ux_recv.at[2], device(columns[1], v))
+    send(mine, ux_recv.at[3], device(columns[3], v))
     spread(0)
     for q in (1, 2, 3):
         arrived(block(columns[q], v), ux_recv.at[q])
@@ -240,7 +248,7 @@
         write(m, 1).start()
         return carry
 
-    lax.fori_loop(0, channels, channel, 0)
+    lax.fori_loop(0, channels, channel, 0, unroll=True)
     for m in range(channels):
         write(m, 0).wait()
         write(m, 1).wait()
@@ -265,12 +273,14 @@
             pltpu.VMEM((2, inputs, channels), jnp.float32),
             pltpu.VMEM((TAPS, NFFT), jnp.float32),
             pltpu.VMEM((4, 8, NFFT), jnp.float32),
-            pltpu.VMEM((3, 4 * channels, NFFT), jnp.bfloat16),
-            pltpu.VMEM((3, 4 * channels, 8 * inputs), jnp.float32),
-            pltpu.VMEM((fgrp, 7, mine, 2 * inputs), jnp.float32),
-            pltpu.VMEM((fgrp, 7, mine, 2 * inputs), jnp.float32),
+            pltpu.VMEM((12 * channels, NFFT), jnp.bfloat16),
+            pltpu.VMEM((12 * channels, 8 * inputs), jnp.float32),
+            pltpu.VMEM((fgrp, 4, mine, 2 * inputs), jnp.float32),
+            pltpu.VMEM((fgrp, 4, mine, 2 * inputs), jnp.float32),
+            pltpu.VMEM((fgrp, 3, mine, 2 * inputs), jnp.bfloat16),
+            pltpu.VMEM((fgrp, 3, mine, 2 * inputs), jnp.bfloat16),
             pltpu.VMEM((mine, spectra, 2 * inputs), jnp.float32),
-            dma((7,)), dma((fgrp,)), dma((fgrp,)), dma((40,)), dma((4,)), dma((4, 4)), dma((4, 4)),
+            dma((7,)), dma((2, fgrp)), dma((2, fgrp)), dma((40,)), dma((4,)), dma((4, 4)), dma((4, 4)),
         ],
         compiler_params=pltpu.CompilerParams(
             collective_id=0, has_side_effects=True, vmem_limit_bytes=32 * 1024 * 1024

time: 40.9 us -> 38.3 us (0.936)
  Pallas kernels: 40.9 us -> 38.2 us
    pallas_call x1, Pallas kernels: 36.6 us -> 34.4 us  [body(): pl.pallas_call(spectra_kernel, out_shape=pltpu.VMEM((count, mine, spectra...]
    pallas_call x1, Pallas kernels: 4.24 us -> 3.82 us  [body(): pl.pallas_call(functools.partial(correlate_kernel, 1.0 / math.sqrt(spectr...]
where the time goes in v3:
time: 38.3 us
  Pallas kernels  38.2 us (100%)
    pallas_call x1, Pallas kernels, body(): pl.pallas_call(spectra_kernel, out_shape=pltpu.VMEM((count, mine, spectra...  34.4 us
    pallas_call x1, Pallas kernels, body(): pl.pallas_call(functools.partial(correlate_kernel, 1.0 / math.sqrt(spectr...  3.82 us

profile of v3, /device:TPU:1, one launch (start us, length us, event | category | flops | bytes accessed | tf_op | source)
XLA Modules:
  0.0 38.3 jit_solution(6146052867932190615)
XLA Ops:
  0.0 34.4 %spectra.1.blocks = bf16[32,8,32,128]{3,2,1,0:T(8,128)(2,1)S(1)} custom-call(bf16[2,64,16384]{2,1,0:T(8,128)(2,1)} %volt.1, f32[2,64,64]{2,1,0:T(8,128)} %gains.1, f32[4,4096]{1,0:T(4,128)} %constant.4.clone.taps, f32[4,8,4096]{2,1,0:T(8,128)} %constant.5.clone.rot), custom_call_target="tpu_custom_call" | custom-call | tf_op jit(solution)/shard_map/spectra/pallas_call | solution.py:266
  34.4 3.8 %correlate.1 = f32[8,2,64,2048]{3,2,1,0:T(8,128)} custom-call(bf16[32,8,32,128]{3,2,1,0:T(8,128)(2,1)S(1)} %spectra.1.blocks), custom_call_target="tpu_custom_call" | custom-call | tf_op jit(solution)/shard_map/correlate/pallas_call | solution.py:294

commit v4 on v3

--- a/solution.py
+++ b/solution.py
@@ -146,12 +146,14 @@
 
     pl.semaphore_wait(barrier, depth + 6)
     turns = []
-    for dz in (4, 3, 5, 2, 6, 1, 7):
+    for n in range(depth - 1):
+        target = n + jnp.where(z <= n, 1, 0)
+        dz = (target - z + depth) % depth
         for k, (mine, theirs) in enumerate(((wide_send, wide), (thin_send, thin))):
             turn = pltpu.make_async_remote_copy(
-                src_ref=mine.at[ring[dz]], dst_ref=theirs.at[z],
+                src_ref=mine.at[target], dst_ref=theirs.at[z],
                 send_sem=a2a_send.at[k, dz], recv_sem=a2a_recv.at[k, dz],
-                device_id={"fgrp": ring[dz], "tile": tile, "pol": pol}, device_id_type=MESH,
+                device_id={"fgrp": target, "tile": tile, "pol": pol}, device_id_type=MESH,
             )
             turn.start()
             turns.append(turn)
@@ -193,14 +195,17 @@
 
     def spread(q):
         b = block(columns[q], v)
+        send(b, vy_recv.at[q, 3], device(u, rows[3]))
         send(b, vy_recv.at[q, 1], device(u, rows[2]))
         send(b, vy_recv.at[q, 2], device(u, rows[1]))
-        send(b, vy_recv.at[q, 3], device(u, rows[3]))
-        send(b, pt_recv.at[q, 0], partner)
+        if q:
+            send(b, pt_recv.at[q, 0], partner)
 
     send(mine, ux_recv.at[1], device(columns[2], v))
     send(mine, ux_recv.at[2], device(columns[1], v))
     send(mine, ux_recv.at[3], device(columns[3], v))
+    send(mine, pt_recv.at[0, 0], partner)
+    arrived(mine, pt_recv.at[0, 0])
     spread(0)
     for q in (1, 2, 3):
         arrived(block(columns[q], v), ux_recv.at[q])
@@ -212,7 +217,8 @@
             send(b, pt_recv.at[q, r], partner)
     for q in range(4):
         for r in range(4):
-            arrived(mine, pt_recv.at[q, r])
+            if q or r:
+                arrived(mine, pt_recv.at[q, r])
     for turn in turns:
         turn.wait_send()
     for copy in started:

time: 38.3 us -> 37 us (0.966)
  Pallas kernels: 38.2 us -> 36.9 us
    pallas_call x1, Pallas kernels: 34.4 us -> 33.1 us  [body(): pl.pallas_call(spectra_kernel, out_shape=pltpu.VMEM((count, mine, spectra...]
where the time goes in v4:
time: 37 us; the launch traced here: 36.9 us
  Pallas kernels  36.9 us (100%)
    pallas_call x1, Pallas kernels, body(): pl.pallas_call(spectra_kernel, out_shape=pltpu.VMEM((count, mine, spectra...  33.1 us
    pallas_call x1, Pallas kernels, body(): pl.pallas_call(functools.partial(correlate_kernel, 1.0 / math.sqrt(spectr...  3.82 us

profile of v4, /device:TPU:1, one launch (start us, length us, event | category | flops | bytes accessed | tf_op | source)
XLA Modules:
  0.0 36.9 jit_solution(4732913509759020715)
XLA Ops:
  0.0 33.1 %spectra.1.blocks = bf16[32,8,32,128]{3,2,1,0:T(8,128)(2,1)S(1)} custom-call(bf16[2,64,16384]{2,1,0:T(8,128)(2,1)} %volt.1, f32[2,64,64]{2,1,0:T(8,128)} %gains.1, f32[4,4096]{1,0:T(4,128)} %constant.4.clone.taps, f32[4,8,4096]{2,1,0:T(8,128)} %constant.5.clone.rot), custom_call_target="tpu_custom_call" | custom-call | tf_op jit(solution)/shard_map/spectra/pallas_call | solution.py:272
  33.1 3.8 %correlate.1 = f32[8,2,64,2048]{3,2,1,0:T(8,128)} custom-call(bf16[32,8,32,128]{3,2,1,0:T(8,128)(2,1)S(1)} %spectra.1.blocks), custom_call_target="tpu_custom_call" | custom-call | tf_op jit(solution)/shard_map/correlate/pallas_call | solution.py:300

commit v5 on v4

--- a/solution.py
+++ b/solution.py
@@ -149,9 +149,9 @@
     for n in range(depth - 1):
         target = n + jnp.where(z <= n, 1, 0)
         dz = (target - z + depth) % depth
-        for k, (mine, theirs) in enumerate(((wide_send, wide), (thin_send, thin))):
+        for k, (ours, theirs) in enumerate(((wide_send, wide), (thin_send, thin))):
             turn = pltpu.make_async_remote_copy(
-                src_ref=mine.at[target], dst_ref=theirs.at[z],
+                src_ref=ours.at[target], dst_ref=theirs.at[z],
                 send_sem=a2a_send.at[k, dz], recv_sem=a2a_recv.at[k, dz],
                 device_id={"fgrp": target, "tile": tile, "pol": pol}, device_id_type=MESH,
             )
@@ -159,66 +159,94 @@
             turns.append(turn)
     wide[z] = wide_send[z]
     thin[z] = thin_send[z]
-    for turn in turns:
-        turn.wait_recv()
-
     def partial(d, j):
         if j in thin_of:
             return thin[d, thin_of[j]].astype(jnp.float32)
         return wide[d, wide_of[j]]
 
-    for d in range(depth):
-        for j in range(4):
-            value = partial(d, j)
-            if d > 0 and j < 3:
-                value = value + partial(d - 1, j + 4)
-            own[:, 4 * d + j, :] = value
     mine = block(u, v)
-    out[mine] = own[...].astype(jnp.bfloat16)
+    half = depth // 2
+
+    def landed(source):
+        for k, ref in enumerate((wide, thin)):
+            pltpu.make_async_remote_copy(
+                src_ref=ref.at[source], dst_ref=ref.at[source], send_sem=a2a_send.at[k, 0],
+                recv_sem=a2a_recv.at[k, (z - source + depth) % depth],
+                device_id=partner, device_id_type=MESH,
+            ).wait_recv()
+
+    def finish(h):
+        for source in range(h * half, (h + 1) * half):
+            pl.when(z != source)(functools.partial(landed, source))
+        for n in range(half):
+            d = h * half + n
+            for j in range(4):
+                value = partial(d, j)
+                if d > 0 and j < 3:
+                    value = value + partial(d - 1, j + 4)
+                own[h, :, 4 * n + j, :] = value
+        out[mine, h] = own[h].astype(jnp.bfloat16)
 
     started = []
     columns, rows = [u, (u + 3) % 4, (u + 1) % 4, (u + 2) % 4], [v, (v + 3) % 4, (v + 1) % 4, (v + 2) % 4]
 
-    def send(b, recv_sem, to):
+    def send(b, h, recv_sem, to):
         copy = pltpu.make_async_remote_copy(
-            src_ref=out.at[b], dst_ref=out.at[b], send_sem=ag_send.at[len(started)],
+            src_ref=out.at[b, h], dst_ref=out.at[b, h], send_sem=ag_send.at[len(started)],
             recv_sem=recv_sem, device_id=to, device_id_type=MESH,
         )
         copy.start()
         started.append(copy)
 
-    def arrived(b, recv_sem):
+    def arrived(b, h, recv_sem):
         pltpu.make_async_remote_copy(
-            src_ref=out.at[b], dst_ref=out.at[b], send_sem=ag_send.at[0],
+            src_ref=out.at[b, h], dst_ref=out.at[b, h], send_sem=ag_send.at[0],
             recv_sem=recv_sem, device_id=partner, device_id_type=MESH,
         ).wait_recv()
 
-    def spread(q):
+    def along_u(h):
+        send(mine, h, ux_recv.at[h, 1], device(columns[2], v))
+        send(mine, h, ux_recv.at[h, 2], device(columns[1], v))
+        send(mine, h, ux_recv.at[h, 3], device(columns[3], v))
+        send(mine, h, pt_recv.at[h, 0, 0], partner)
+
+    def along_v(h, q):
         b = block(columns[q], v)
-        send(b, vy_recv.at[q, 3], device(u, rows[3]))
-        send(b, vy_recv.at[q, 1], device(u, rows[2]))
-        send(b, vy_recv.at[q, 2], device(u, rows[1]))
-        if q:
-            send(b, pt_recv.at[q, 0], partner)
-
-    send(mine, ux_recv.at[1], device(columns[2], v))
-    send(mine, ux_recv.at[2], device(columns[1], v))
-    send(mine, ux_recv.at[3], device(columns[3], v))
-    send(mine, pt_recv.at[0, 0], partner)
-    arrived(mine, pt_recv.at[0, 0])
-    spread(0)
-    for q in (1, 2, 3):
-        arrived(block(columns[q], v), ux_recv.at[q])
-        spread(q)
-    for q in range(4):
+        send(b, h, vy_recv.at[h, q, 3], device(u, rows[3]))
+        send(b, h, vy_recv.at[h, q, 1], device(u, rows[2]))
+        send(b, h, vy_recv.at[h, q, 2], device(u, rows[1]))
+
+    def column(h, q):
+        b = block(columns[q], v)
+        arrived(b, h, ux_recv.at[h, q])
+        along_v(h, q)
+        send(b, h, pt_recv.at[h, q, 0], partner)
+
+    def share(h, q):
         for r in (1, 2, 3):
             b = block(columns[q], rows[r])
-            arrived(b, vy_recv.at[q, r])
-            send(b, pt_recv.at[q, r], partner)
+            arrived(b, h, vy_recv.at[h, q, r])
+            send(b, h, pt_recv.at[h, q, r], partner)
+
+    finish(0)
+    along_u(0)
+    along_v(0, 0)
+    finish(1)
+    along_u(1)
+    for q in (1, 2, 3):
+        column(0, q)
+    along_v(1, 0)
+    share(0, 0)
+    for q in (1, 2, 3):
+        column(1, q)
+    for q in (1, 2, 3):
+        share(0, q)
     for q in range(4):
-        for r in range(4):
-            if q or r:
-                arrived(mine, pt_recv.at[q, r])
+        share(1, q)
+    for h in range(2):
+        for q in range(4):
+            for r in range(4):
+                arrived(mine, h, pt_recv.at[h, q, r])
     for turn in turns:
         turn.wait_send()
     for copy in started:
@@ -227,20 +255,23 @@
 
 def correlate_kernel(norm, blocks, out, vis, sems):
     mine = lax.axis_index("tile") * 2 + lax.axis_index("pol")
-    count, channels = blocks.shape[0], blocks.shape[1]
+    count, channels = blocks.shape[0], blocks.shape[2]
     first = lax.broadcasted_iota(jnp.int32, (32, 128), 1) < 64
 
     def write(m, part):
         return pltpu.make_async_copy(vis.at[m, part], out.at[m, part], sems.at[m, part])
 
+    def spectra(b, m):
+        return jnp.concatenate([blocks[b, 0, m], blocks[b, 1, m]], axis=0)
+
     def channel(m, carry):
-        a = blocks[mine, m]
+        a = spectra(mine, m)
         swapped = swap_halves(a)
         lhs = jnp.concatenate([a, jnp.where(first, swapped, -swapped)], axis=0)
         for q in range(0, count, 4):
             tiles = []
             for b in (q, q + 2):
-                g, h = blocks[b, m], blocks[b + 1, m]
+                g, h = spectra(b, m), spectra(b + 1, m)
                 re = jnp.where(first, g, swap_halves(h))
                 im = jnp.where(first, swap_halves(g), h)
                 tiles.append(jnp.concatenate([re, im], axis=0))
@@ -271,7 +302,7 @@
     dma = pltpu.SemaphoreType.DMA
     blocks = pl.pallas_call(
         spectra_kernel,
-        out_shape=pltpu.VMEM((count, mine, spectra, 2 * inputs), jnp.bfloat16),
+        out_shape=pltpu.VMEM((count, 2, mine, spectra // 2, 2 * inputs), jnp.bfloat16),
         in_specs=[any_spec] * 4,
         out_specs=vmem_spec,
         scratch_shapes=[
@@ -285,8 +316,8 @@
             pltpu.VMEM((fgrp, 4, mine, 2 * inputs), jnp.float32),
             pltpu.VMEM((fgrp, 3, mine, 2 * inputs), jnp.bfloat16),
             pltpu.VMEM((fgrp, 3, mine, 2 * inputs), jnp.bfloat16),
-            pltpu.VMEM((mine, spectra, 2 * inputs), jnp.float32),
-            dma((7,)), dma((2, fgrp)), dma((2, fgrp)), dma((40,)), dma((4,)), dma((4, 4)), dma((4, 4)),
+            pltpu.VMEM((2, mine, spectra // 2, 2 * inputs), jnp.float32),
+            dma((7,)), dma((2, fgrp)), dma((2, fgrp)), dma((64,)), dma((2, 4)), dma((2, 4, 4)), dma((2, 4, 4)),
         ],
         compiler_params=pltpu.CompilerParams(
             collective_id=0, has_side_effects=True, vmem_limit_bytes=32 * 1024 * 1024

time: 37 us -> 35.6 us (0.962)
  Pallas kernels: 36.9 us -> 35.5 us
    pallas_call x1, Pallas kernels: 33.1 us -> 31.7 us  [body(): pl.pallas_call(spectra_kernel, out_shape=pltpu.VMEM((count, 2, mine, spec...]
where the time goes in v5:
time: 35.6 us; the launch traced here: 35.5 us
  Pallas kernels  35.5 us (100%)
    pallas_call x1, Pallas kernels, body(): pl.pallas_call(spectra_kernel, out_shape=pltpu.VMEM((count, 2, mine, spec...  31.7 us
    pallas_call x1, Pallas kernels, body(): pl.pallas_call(functools.partial(correlate_kernel, 1.0 / math.sqrt(spectr...  3.82 us

profile of v5, /device:TPU:1, one launch (start us, length us, event | category | flops | bytes accessed | tf_op | source)
XLA Modules:
  0.0 35.5 jit_solution(14481918377867044744)
XLA Ops:
  0.0 31.7 %spectra.1.blocks = bf16[32,2,8,16,128]{4,3,2,1,0:T(8,128)(2,1)S(1)} custom-call(bf16[2,64,16384]{2,1,0:T(8,128)(2,1)} %volt.1, f32[2,64,64]{2,1,0:T(8,128)} %gains.1, f32[4,4096]{1,0:T(4,128)} %constant.4.clone.taps, f32[4,8,4096]{2,1,0:T(8,128)} %constant.5.clone.rot), custom_call_target="tpu_custom_call" | custom-call | tf_op jit(solution)/shard_map/spectra/pallas_call | solution.py:303
  31.7 3.8 %correlate.1 = f32[8,2,64,2048]{3,2,1,0:T(8,128)} custom-call(bf16[32,2,8,16,128]{4,3,2,1,0:T(8,128)(2,1)S(1)} %spectra.1.blocks), custom_call_target="tpu_custom_call" | custom-call | tf_op jit(solution)/shard_map/correlate/pallas_call | solution.py:331

commit v6 on v5

--- a/solution.py
+++ b/solution.py
@@ -64,6 +64,8 @@
 
     barrier = pltpu.get_barrier_semaphore()
     plane_peers = [device((u + d) % 4, v) for d in (1, 2, 3)] + [device(u, (v + d) % 4) for d in (1, 2, 3)]
+    plane_peers += [device((u + 2) % 4, (v + d) % 4) for d in (1, 2, 3)]
+    plane_peers += [device((u + d) % 4, (v + 2) % 4) for d in (1, 3)]
     plane_peers.append(partner)
     for peer in plane_peers:
         pl.semaphore_signal(barrier, inc=1, device_id=peer, device_id_type=MESH)
@@ -113,6 +115,10 @@
         return carry
 
     lax.fori_loop(0, NFFT // lanes, make, 0)
+    lane = lax.broadcasted_iota(jnp.int32, (64, 128), 1)
+    sign = jnp.where(lane < 64, 1.0, -1.0).astype(jnp.float32)
+    g_re = jnp.transpose(jnp.concatenate([gbuf[0], gbuf[0]], axis=0))
+    g_im = jnp.transpose(jnp.concatenate([gbuf[1], gbuf[1]], axis=0)) * -sign
     for copy in frames:
         copy.wait()
     acc[...] = lax.dot_general(
@@ -120,10 +126,6 @@
         preferred_element_type=jnp.float32,
     )
 
-    lane = lax.broadcasted_iota(jnp.int32, (64, 128), 1)
-    sign = jnp.where(lane < 64, 1.0, -1.0).astype(jnp.float32)
-    g_re = jnp.transpose(jnp.concatenate([gbuf[0], gbuf[0]], axis=0))
-    g_im = jnp.transpose(jnp.concatenate([gbuf[1], gbuf[1]], axis=0)) * -sign
     thin_of, wide_of = {0: 0, 3: 1, 6: 2}, {1: 0, 2: 1, 4: 2, 5: 3}
     for j in range(7):
         total = None
@@ -144,7 +146,7 @@
             else:
                 wide_send[c, wide_of[j]] = gained[8 * c : 8 * c + 8]
 
-    pl.semaphore_wait(barrier, depth + 6)
+    pl.semaphore_wait(barrier, depth + 11)
     turns = []
     for n in range(depth - 1):
         target = n + jnp.where(z <= n, 1, 0)
@@ -212,14 +214,23 @@
 
     def along_v(h, q):
         b = block(columns[q], v)
-        send(b, h, vy_recv.at[h, q, 3], device(u, rows[3]))
+        if h == 0 or q == 0:
+            send(b, h, vy_recv.at[h, q, 3], device(u, rows[3]))
         send(b, h, vy_recv.at[h, q, 1], device(u, rows[2]))
         send(b, h, vy_recv.at[h, q, 2], device(u, rows[1]))
+
+    def across(h):
+        send(mine, h, vy_recv.at[h, 3, 3], device(columns[3], rows[3]))
+        send(mine, h, vy_recv.at[h, 3, 1], device(columns[3], rows[2]))
+        send(mine, h, vy_recv.at[h, 3, 2], device(columns[3], rows[1]))
+        send(mine, h, vy_recv.at[h, 1, 3], device(columns[2], rows[3]))
+        send(mine, h, vy_recv.at[h, 2, 3], device(columns[1], rows[3]))
 
     def column(h, q):
         b = block(columns[q], v)
         arrived(b, h, ux_recv.at[h, q])
-        along_v(h, q)
+        if h == 0 or q < 3:
+            along_v(h, q)
         send(b, h, pt_recv.at[h, q, 0], partner)
 
     def share(h, q):
@@ -233,6 +244,7 @@
     along_v(0, 0)
     finish(1)
     along_u(1)
+    across(1)
     for q in (1, 2, 3):
         column(0, q)
     along_v(1, 0)

time: 35.6 us -> 34.8 us (0.978)
  Pallas kernels: 35.5 us -> 34.7 us
    pallas_call x1, Pallas kernels: 31.7 us -> 30.9 us  [body(): pl.pallas_call(spectra_kernel, out_shape=pltpu.VMEM((count, 2, mine, spec...]
where the time goes in v6:
time: 34.8 us; the launch traced here: 34.7 us
  Pallas kernels  34.7 us (100%)
    pallas_call x1, Pallas kernels, body(): pl.pallas_call(spectra_kernel, out_shape=pltpu.VMEM((count, 2, mine, spec...  30.9 us
    pallas_call x1, Pallas kernels, body(): pl.pallas_call(functools.partial(correlate_kernel, 1.0 / math.sqrt(spectr...  3.82 us

profile of v6, /device:TPU:1, one launch (start us, length us, event | category | flops | bytes accessed | tf_op | source)
XLA Modules:
  0.0 34.7 jit_solution(1104867362290975773)
XLA Ops:
  0.0 30.9 %spectra.1.blocks = bf16[32,2,8,16,128]{4,3,2,1,0:T(8,128)(2,1)S(1)} custom-call(bf16[2,64,16384]{2,1,0:T(8,128)(2,1)} %volt.1, f32[2,64,64]{2,1,0:T(8,128)} %gains.1, f32[4,4096]{1,0:T(4,128)} %constant.4.clone.taps, f32[4,8,4096]{2,1,0:T(8,128)} %constant.5.clone.rot), custom_call_target="tpu_custom_call" | custom-call | tf_op jit(solution)/shard_map/spectra/pallas_call | solution.py:315
  30.9 3.8 %correlate.1 = f32[8,2,64,2048]{3,2,1,0:T(8,128)} custom-call(bf16[32,2,8,16,128]{4,3,2,1,0:T(8,128)(2,1)S(1)} %spectra.1.blocks), custom_call_target="tpu_custom_call" | custom-call | tf_op jit(solution)/shard_map/correlate/pallas_call | solution.py:343

commit v7 on v6

--- a/solution.py
+++ b/solution.py
@@ -233,8 +233,8 @@
             along_v(h, q)
         send(b, h, pt_recv.at[h, q, 0], partner)
 
-    def share(h, q):
-        for r in (1, 2, 3):
+    def share(h, q, offsets=(1, 2, 3)):
+        for r in offsets:
             b = block(columns[q], rows[r])
             arrived(b, h, vy_recv.at[h, q, r])
             send(b, h, pt_recv.at[h, q, r], partner)
@@ -253,8 +253,12 @@
         column(1, q)
     for q in (1, 2, 3):
         share(0, q)
-    for q in range(4):
-        share(1, q)
+    share(1, 0)
+    share(1, 3)
+    for q in (1, 2):
+        share(1, q, (3,))
+    for q in (1, 2):
+        share(1, q, (1, 2))
     for h in range(2):
         for q in range(4):
             for r in range(4):

time: 34.8 us -> 34.6 us (level)
  no operation moved by 1% of the time
where the time goes in v7:
time: 34.6 us; the launch traced here: 34.5 us
  Pallas kernels  34.5 us (100%)
    pallas_call x1, Pallas kernels, body(): pl.pallas_call(spectra_kernel, out_shape=pltpu.VMEM((count, 2, mine, spec...  30.7 us
    pallas_call x1, Pallas kernels, body(): pl.pallas_call(functools.partial(correlate_kernel, 1.0 / math.sqrt(spectr...  3.82 us

profile of v7, /device:TPU:1, one launch (start us, length us, event | category | flops | bytes accessed | tf_op | source)
XLA Modules:
  0.0 34.5 jit_solution(4752230179641934615)
XLA Ops:
  0.0 30.7 %spectra.1.blocks = bf16[32,2,8,16,128]{4,3,2,1,0:T(8,128)(2,1)S(1)} custom-call(bf16[2,64,16384]{2,1,0:T(8,128)(2,1)} %volt.1, f32[2,64,64]{2,1,0:T(8,128)} %gains.1, f32[4,4096]{1,0:T(4,128)} %constant.4.clone.taps, f32[4,8,4096]{2,1,0:T(8,128)} %constant.5.clone.rot), custom_call_target="tpu_custom_call" | custom-call | tf_op jit(solution)/shard_map/spectra/pallas_call | solution.py:319
  30.7 3.8 %correlate.1 = f32[8,2,64,2048]{3,2,1,0:T(8,128)} custom-call(bf16[32,2,8,16,128]{4,3,2,1,0:T(8,128)(2,1)S(1)} %spectra.1.blocks), custom_call_target="tpu_custom_call" | custom-call | tf_op jit(solution)/shard_map/correlate/pallas_call | solution.py:347
